TPU v7x, 512 devices: a whole 4x4x16 slice. The times are simulated.
512 devices in a mesh: chain: 64 (over x, y, z_hi, core), block: 8 (over z_lo).
Axes of the slice: x: 4, y: 4, z: 16 (z_hi: 2, z_lo: 8; z = z_hi * 8 + z_lo), core: 2. Of those that a mesh axis runs over, the one named last changes fastest.
Arguments:
- site_tensors: bfloat16 [64, 32, 2, 256, 256], P('chain', 'block'), may hold values from -4.5 to 7.5
- sketch: bfloat16 [512, 256], replicated, may hold values from -6 to 6
- bond_sizes: int32 [64, 2, 32], P('chain'), may hold values from 32 to 256, as said below
- kept_ranks: int32 [64, 2, 32], P('chain'), may hold values from 0 to 256, as said below
- couplings: float32 [64, 2, 3], P('chain'), may hold values from -1 to 2.5, as said below
Outputs:
- updated_sites: bfloat16 [64, 32, 2, 256, 256], P('chain', 'block')
Inputs may be any that keep to these rules, and one draw needn't show every extreme that they name: bond_sizes[i, 1] are the block sizes of the bond right of site i and bond_sizes[i, 0] equals bond_sizes[i - 1 mod 64, 1]; every bond has a block of exactly 256. kept_ranks[i, 1] belongs to the bond right of site i and kept_ranks[i, 0] equals kept_ranks[i - 1 mod 64, 1]; a count never exceeds that block's size; some block keeps exactly 256. couplings[i, 0] equals couplings[i - 1 mod 64, 1]; hopping lies in 0.5 to 2.5, the other two in -1 to 1.
All inputs are finite; a program needn't handle non-finite values.
Results may differ from a plain program's by a relative error of at most 0.035.
Values may be sent and summed in bfloat16 or wider, within the bound.
A program may use at most 64 MiB of HBM per device.

v0:
```python
import functools
import math

import jax
import jax.numpy as jnp
from jax import lax
from jax.experimental import pallas as pl
from jax.experimental.pallas import tpu as pltpu
from jax.sharding import PartitionSpec as P

tau_step = 0.5
NN = (((1,), (0,)), ((), ()))
NT = (((1,), (1,)), ((), ()))


def mm(x, y, dims=NN):
    return lax.dot_general(x, y, dims, preferred_element_type=jnp.float32)


def split(x):
    high = x.astype(jnp.bfloat16)
    low = (x - high.astype(jnp.float32)).astype(jnp.bfloat16)
    return high, low


def mm3(x, y, dims=NN):
    x_high, x_low = split(x)
    y_high, y_low = split(y)
    return mm(x_high, y_high, dims) + (mm(x_high, y_low, dims) + mm(x_low, y_high, dims))


def inv_factors(blocks):
    nb = blocks[0].shape[0]
    ngr = nb // 8
    eye = (lax.broadcasted_iota(jnp.int32, (nb, nb), 0) == lax.broadcasted_iota(jnp.int32, (nb, nb), 1)).astype(jnp.float32)
    work = []
    for g in blocks:
        full = jnp.concatenate([g, eye], axis=1)
        work.append([full[8 * i: 8 * i + 8, :] for i in range(ngr)])
    lane = lax.broadcasted_iota(jnp.int32, (8, 2 * nb), 1)
    sub = lax.broadcasted_iota(jnp.int32, (8, 2 * nb), 0)
    for j in range(nb):
        gj, sj = j // 8, j % 8
        for w in work:
            row = w[gj][sj: sj + 1, :]
            piv = row[:, j: j + 1]
            t = row * (1.0 / piv)
            tb = jnp.broadcast_to(t, (8, 2 * nb))
            for i in range(gj, ngr):
                if i == gj and sj == 7:
                    continue
                c = jnp.broadcast_to(w[i][:, j: j + 1], (8, 2 * nb))
                if i == gj:
                    c = jnp.where(sub > sj, c, 0.0)
                w[i] = w[i] - c * tb
    out = []
    for w in work:
        rows = []
        for i in range(ngr):
            d = jnp.sum(jnp.where(lane == sub + 8 * i, w[i], 0.0), axis=1, keepdims=True)
            rows.append(w[i] * lax.rsqrt(d))
        full = jnp.concatenate(rows, axis=0)
        out.append(full[:, nb:])
    return out

def inv_cholesky(w_refs, nb=64, mmf=mm3):
    n = w_refs[0].shape[-1]
    for k in range(n // nb):
        lo, hi = k * nb, (k + 1) * nb
        xs = inv_factors([w[lo:hi, lo:hi] for w in w_refs])
        for w, x in zip(w_refs, xs):
            if hi < n:
                panel = mmf(w[hi:, lo:hi], x, NT)
                right = mmf(x, w[lo:hi, hi:])
            if lo > 0:
                left = jnp.concatenate([mmf(x, w[lo:hi, :lo]), x], axis=1)
            else:
                left = x
            w[lo:hi, :hi] = left
            if hi < n:
                w[lo:hi, hi:] = jnp.zeros((nb, n - hi), jnp.float32)
                w[hi:, hi:] = w[hi:, hi:] - mmf(panel, right)
                upd = mmf(panel, left)
                if lo > 0:
                    w[hi:, :lo] = w[hi:, :lo] - upd[:, :lo]
                w[hi:, lo:hi] = -upd[:, lo:]


MESH = pl.DeviceIdType.MESH
VMEM = pl.BlockSpec(memory_space=pltpu.VMEM)


def gate_terms(coupling):
    hopping = coupling[0]
    ising_term = coupling[1]
    field_term = coupling[2]
    rotation = 0.5 * tau_step * hopping
    middle_scale = jnp.exp(0.25 * tau_step * ising_term)
    weight_empty = jnp.exp(-tau_step * (0.25 * ising_term - 0.5 * field_term))
    weight_full = jnp.exp(-tau_step * (0.25 * ising_term + 0.5 * field_term))
    weight_stay = middle_scale * jnp.cosh(rotation)
    weight_swap = -middle_scale * jnp.sinh(rotation)
    return jnp.stack([weight_empty, weight_stay, weight_swap, weight_full])


def update_sectors(left, top, low, bdims, sketch_t, ranks, weights, basis_ref, coef_ref, part_ref, scratch, sent):
    two_ref, sample_ref, tri_refs = scratch
    w_empty, w_stay, w_swap, w_full = weights
    size = sample_ref.shape[1]

    def product(x, y):
        return mm(x, y, bdims).astype(jnp.bfloat16).astype(jnp.float32)

    up_stay = product(left(0, 1), top(0))
    stay_up = product(left(0, 0), low(0))
    for i in range(2):
        up_up = product(left(i, 1), low(i + 1))
        two_ref[i, size:, :size] = (w_swap * stay_up + w_stay * up_stay).astype(jnp.bfloat16)
        two_ref[i, size:, size:] = (w_full * up_up).astype(jnp.bfloat16)
        stay_stay = product(left(i + 1, 0), top(i))
        stay_up = product(left(i + 1, 0), low(i + 1))
        up_stay = product(left(i + 1, 1), top(i + 1))
        two_ref[i, :size, :size] = (w_empty * stay_stay).astype(jnp.bfloat16)
        two_ref[i, :size, size:] = (w_stay * stay_up + w_swap * up_stay).astype(jnp.bfloat16)
    row = lax.broadcasted_iota(jnp.int32, (size, size), 0)
    column = lax.broadcasted_iota(jnp.int32, (size, size), 1)
    row_wide = lax.broadcasted_iota(jnp.int32, (size, 2 * size), 0)
    for i in range(2):
        sample = mm(sketch_t[...], two_ref[i], NT)
        sample = jnp.where(row_wide.astype(jnp.float32) < ranks[i], sample, 0.0)
        sample_ref[i] = sample
        high, low_part = split(sample)
        cross = mm(high, low_part, NT)
        gram = mm(high, high, NT) + (cross + cross.T)
        free = (row == column) & (row.astype(jnp.float32) >= ranks[i])
        tri_refs[i][...] = gram + jnp.where(free, 1.0, 0.0)
    inv_cholesky(tri_refs)
    total = jnp.zeros((1, 1), jnp.float32)
    for i in range(2):
        basis = mm3(tri_refs[i][...], sample_ref[i]) * math.sqrt(size)
        basis_ref[i] = basis.astype(jnp.bfloat16)
    for i in range(2):
        coef = mm(basis_ref[i], two_ref[i])
        total = total + jnp.sum(jnp.sum(coef * coef, axis=1, keepdims=True), axis=0, keepdims=True)
        coef_ref[i] = coef.astype(jnp.bfloat16)
        sent(i)
    part_ref[...] = jnp.broadcast_to(total, part_ref.shape)


def signal_to(semaphore, chain, block):
    pl.semaphore_signal(semaphore, inc=1, device_id={"chain": chain, "block": block}, device_id_type=MESH)


def entry_kernel(blocks, own, row, other, outer, lower, sib_row, send_sems, recv_sems):
    chain = lax.axis_index("chain")
    block = lax.axis_index("block")
    side = lax.rem(chain, 2)
    sib = chain + 1 - 2 * side
    has_prev = block > 0
    has_next = block < blocks - 1
    even = side == 0
    odd = side == 1
    barrier = pltpu.get_barrier_semaphore()
    signal_to(barrier, sib, block)
    pl.when(has_next)(lambda: signal_to(barrier, chain, block + 1))
    pl.when(has_prev)(lambda: signal_to(barrier, chain, block - 1))
    pl.when(even & has_prev)(lambda: signal_to(barrier, sib, block - 1))
    pl.when(odd & has_next)(lambda: signal_to(barrier, sib, block + 1))
    prev_count = has_prev.astype(jnp.int32)
    next_count = has_next.astype(jnp.int32)
    pl.semaphore_wait(barrier, 1 + (2 - side) * prev_count + (1 + side) * next_count)

    def remote(src, dst, k, to_chain, to_block):
        return pltpu.make_async_remote_copy(
            src_ref=src,
            dst_ref=dst,
            send_sem=send_sems.at[k],
            recv_sem=recv_sems.at[k],
            device_id={"chain": to_chain, "block": to_block},
            device_id_type=MESH,
        )

    edge_next = remote(own.at[3], outer, 0, chain, block + 1)
    edge_prev = remote(own.at[0], outer, 0, chain, block - 1)
    edge_low = remote(own.at[3, 1], lower, 1, sib, block + 1)
    to_odd = remote(own.at[pl.ds(1, 3)], other, 2, sib, block)
    to_even = remote(own.at[pl.ds(0, 3)], other, 2, sib, block)
    rows = remote(row, sib_row, 3, sib, block)
    pl.when(even & has_next)(edge_next.start)
    pl.when(odd & has_prev)(edge_prev.start)
    pl.when(odd & has_next)(edge_low.start)
    rows.start()
    pl.when(even)(to_odd.start)
    pl.when(odd)(to_even.start)

    @pl.when((even & (block == 0)) | (odd & (block == blocks - 1)))
    def _():
        outer[...] = jnp.zeros_like(outer)

    @pl.when(odd | (block == 0))
    def _():
        lower[...] = jnp.zeros_like(lower)

    rows.wait()
    to_odd.wait()
    pl.when((even & has_prev) | (odd & has_next))(edge_next.wait_recv)
    pl.when((even & has_next) | (odd & has_prev))(edge_next.wait_send)
    pl.when(even & has_prev)(edge_low.wait_recv)
    pl.when(odd & has_next)(edge_low.wait_send)


def step_kernel(chips, blocks, target, even_row, odd_row, own, other, outer, lower, sketch_t, out, *refs):
    (left_ref, top_ref, low_ref, two_ref, sample_ref, tri_a, tri_b, basis_ref, coef_ref, far_ref, edge_ref) = refs[:11]
    (new_ref, sib_ref, bot_ref, part_ref, norm_ref, sum_ref, scale_ref, send_sems, recv_sems, nsend, nrecv) = refs[11:]
    size = bot_ref.shape[0]
    chain = lax.axis_index("chain")
    block = lax.axis_index("block")
    side = lax.rem(chain, 2)
    sib = chain + 1 - 2 * side
    sites = 2 * chips
    has_prev = block > 0
    has_next = block < blocks - 1
    even = side == 0
    odd = side == 1
    back = lax.rem(chain + sites - 2, sites)
    ahead = lax.rem(chain + 2, sites)
    ahead_even = lax.rem(chain + 2 - side, sites)
    back_odd = lax.rem(chain + sites - 1, sites)
    group = 2 * blocks
    me = side * blocks + block
    barrier = pltpu.get_barrier_semaphore()

    def peer(step):
        index = lax.rem(me + step, group)
        return index, chain - side + index // blocks, lax.rem(index, blocks)

    for step in range(1, group):
        _, to_chain, to_block = peer(step)
        signal_to(barrier, to_chain, to_block)
    signal_to(barrier, back, block)

    @pl.when(even)
    def _():
        signal_to(barrier, back_odd, block)
        signal_to(barrier, ahead, block)

    @pl.when(odd)
    def _():
        signal_to(barrier, ahead, block)
        signal_to(barrier, ahead_even, block)

    def remote(src, dst, k, to_chain, to_block):
        return pltpu.make_async_remote_copy(
            src_ref=src,
            dst_ref=dst,
            send_sem=send_sems.at[k],
            recv_sem=recv_sems.at[k],
            device_id={"chain": to_chain, "block": to_block},
            device_id_type=MESH,
        )

    def norm_copy(layer, step):
        index, to_chain, to_block = peer(step)
        return pltpu.make_async_remote_copy(
            src_ref=norm_ref.at[layer, me],
            dst_ref=norm_ref.at[layer, me],
            send_sem=nsend.at[layer, step],
            recv_sem=nrecv.at[layer, me],
            device_id={"chain": to_chain, "block": to_block},
            device_id_type=MESH,
        )

    def norm_arrival(layer, step):
        index, to_chain, to_block = peer(step)
        return pltpu.make_async_remote_copy(
            src_ref=norm_ref.at[layer, index],
            dst_ref=norm_ref.at[layer, index],
            send_sem=nsend.at[layer, step],
            recv_sem=nrecv.at[layer, index],
            device_id={"chain": to_chain, "block": to_block},
            device_id_type=MESH,
        )

    def share_norm(layer):
        norm_ref[layer, me] = part_ref[...]
        for step in range(1, group):
            norm_copy(layer, step).start()

    def norm_scale(layer):
        for step in range(1, group):
            norm_arrival(layer, step).wait_recv()
        total = norm_ref[layer, 0]
        for i in range(1, group):
            total = total + norm_ref[layer, i]
        return jnp.sqrt(target / total)

    @pl.when(even)
    def _():
        left_ref[0] = outer[...]
        left_ref[1] = own[0]
        left_ref[2] = own[1]
        low_ref[0] = lower[...]
        for i in range(3):
            top_ref[i] = other[i, 0]
        for i in range(2):
            low_ref[i + 1] = other[i, 1]

    @pl.when(odd)
    def _():
        for i in range(3):
            left_ref[i] = other[i]
            low_ref[i] = own[i + 1, 1]
        for i in range(2):
            top_ref[i] = own[i + 2, 0]
        top_ref[2] = outer[0]

    @pl.when(even & (block == 0))
    def _():
        edge_ref[...] = jnp.zeros_like(edge_ref)

    @pl.when(odd & (block == blocks - 1))
    def _():
        far_ref[2] = jnp.zeros_like(far_ref[2])

    @pl.when(odd & (block == blocks - 1))
    def _():
        bot_ref[...] = jnp.zeros_like(bot_ref)

    def row_terms(ref):
        terms = [ref[0:1, i : i + 1] for i in range(8)]
        ranks = [jnp.where(even, terms[i], terms[i + 2]) for i in range(2)]
        return ranks, terms[4:]

    far = [remote(basis_ref.at[0, i], far_ref.at[i], i, back, block) for i in range(2)]
    edge_even = remote(coef_ref.at[0, 1], edge_ref, 2, sib, block)
    edge_odd = remote(coef_ref.at[0, 1], edge_ref, 2, sib, block + 1)
    pass_even = remote(far_ref.at[0], far_ref.at[2], 3, sib, block - 1)
    pass_odd = remote(far_ref.at[0], far_ref.at[2], 3, sib, block)

    def sent_even(i):
        if i == 0:
            pl.semaphore_wait(barrier, group + 2)
            far[0].start()
            far[1].start()
        else:
            pl.when(even)(edge_even.start)
            pl.when(odd & has_next)(edge_odd.start)

    scratch = (two_ref, sample_ref, (tri_a, tri_b))
    ranks, weights = row_terms(even_row)
    update_sectors(
        lambda k, s: left_ref[k, s],
        lambda k: top_ref[k],
        lambda k: low_ref[k],
        NN,
        sketch_t,
        ranks,
        weights,
        basis_ref.at[0],
        coef_ref.at[0],
        part_ref,
        scratch,
        sent_even,
    )
    share_norm(0)
    far[0].wait_recv()
    pl.when(even & has_prev)(pass_even.start)
    pl.when(odd)(pass_odd.start)
    scale = norm_scale(0)[0:1, 0:1]
    pl.when(odd | has_prev)(edge_even.wait_recv)
    far[1].wait_recv()
    pl.when(even | has_next)(pass_even.wait_recv)

    lefts = (edge_ref, coef_ref.at[0, 0], coef_ref.at[0, 1])
    ranks, weights = row_terms(odd_row)
    new_even = [remote(coef_ref.at[1, i], new_ref.at[i], 4 + i, ahead, block) for i in range(2)]
    new_odd = [remote(coef_ref.at[1, i], new_ref.at[2 + i], 6 + i, ahead_even, block) for i in range(2)]
    sibs = [remote(basis_ref.at[1, i], sib_ref.at[i], 8 + i, sib, block) for i in range(2)]
    bot = remote(basis_ref.at[1, 0, :, pl.ds(size, size)], bot_ref, 10, sib, block - 1)

    def sent_odd(i):
        pl.when(even)(new_even[i].start)
        pl.when(odd)(new_odd[i].start)
        pl.when(even)(sibs[i].start)
        if i == 1:
            pl.when(even & has_prev)(bot.start)

    update_sectors(
        lambda k, s: lefts[k][:, s * size : (s + 1) * size],
        lambda k: far_ref[k, :, :size],
        lambda k: far_ref[k, :, size:],
        NT,
        sketch_t,
        ranks,
        [w * scale for w in weights],
        basis_ref.at[1],
        coef_ref.at[1],
        part_ref,
        scratch,
        sent_odd,
    )
    share_norm(1)
    sum_ref[...] = norm_scale(1)
    scale_copy = remote(sum_ref, scale_ref, 11, ahead, block)
    pl.when(even)(scale_copy.start)

    @pl.when(even)
    def _():
        for i in range(2):
            new_even[i].wait_recv()
            new_odd[i].wait_recv()
        scale_copy.wait_recv()
        scale = scale_ref[0:1, 0:1]
        for i in range(4):
            scaled = (new_ref[i].astype(jnp.float32) * scale).astype(jnp.bfloat16)
            out[0, i, 0] = scaled[:, :size]
            out[0, i, 1] = scaled[:, size:]

    @pl.when(odd)
    def _():
        def flip(blocked):
            return blocked.astype(jnp.float32).T.astype(jnp.bfloat16)

        for i in range(2):
            sibs[i].wait_recv()
        pl.when(has_next)(bot.wait_recv)
        for i in range(4):
            basis = sib_ref[i] if i < 2 else basis_ref[1, i - 2]
            out[0, i, 0] = flip(basis[:, :size])
            if i > 0:
                out[0, i - 1, 1] = flip(basis[:, size:])
        out[0, 3, 1] = flip(bot_ref[...])

    for i in range(2):
        far[i].wait_send()
        pl.when(even)(new_even[i].wait_send)
        pl.when(odd)(new_odd[i].wait_send)
        pl.when(even)(sibs[i].wait_send)
    pl.when(even | has_next)(edge_even.wait_send)
    pl.when(odd | has_prev)(pass_even.wait_send)
    pl.when(even & has_prev)(bot.wait_send)
    pl.when(even)(scale_copy.wait_send)
    for layer in range(2):
        for step in range(1, group):
            norm_copy(layer, step).wait_send()


def local_mask(site_block, sizes_row, first_sector):
    sector_count = site_block.shape[0]
    block_width = site_block.shape[-1]
    right_ext = jnp.concatenate([sizes_row[1], jnp.zeros((1,), jnp.int32)])
    left_here = lax.dynamic_slice_in_dim(sizes_row[0], first_sector, sector_count)
    right_here = lax.dynamic_slice_in_dim(right_ext, first_sector, sector_count)
    right_next = lax.dynamic_slice_in_dim(right_ext, first_sector + 1, sector_count)
    row_index = jnp.arange(block_width, dtype=jnp.int32)
    row_keep = row_index[None, :] < left_here[:, None]
    col_stay = row_index[None, :] < right_here[:, None]
    col_next = row_index[None, :] < right_next[:, None]
    keep_zero = row_keep[:, :, None] & col_stay[:, None, :]
    keep_one = row_keep[:, :, None] & col_next[:, None, :]
    keep_both = jnp.stack([keep_zero, keep_one], axis=1)
    return jnp.where(keep_both, site_block, jnp.zeros_like(site_block))


def body(sites, blocks, site_tensors, sketch, bond_sizes, kept_ranks, couplings):
    sector_count = site_tensors.shape[1]
    size = site_tensors.shape[-1]
    bf16 = jnp.bfloat16
    f32 = jnp.float32
    chain = lax.axis_index("chain")
    block = lax.axis_index("block")
    is_left = lax.rem(chain, 2) == 0
    first_sector = block * sector_count

    counts = lax.dynamic_slice_in_dim(kept_ranks[0], first_sector, sector_count, axis=1).astype(f32)
    rows = jnp.concatenate([counts, gate_terms(couplings[0].T).T], axis=1)
    left_row, right_row = (jnp.broadcast_to(jnp.pad(rows[i], (0, 120))[None], (8, 128)) for i in range(2))
    own = local_mask(site_tensors[0], bond_sizes[0], first_sector)

    other, outer, lower, sib_row = pl.pallas_call(
        functools.partial(entry_kernel, blocks),
        out_shape=[
            jax.ShapeDtypeStruct((3, 2, size, size), bf16),
            jax.ShapeDtypeStruct((2, size, size), bf16),
            jax.ShapeDtypeStruct((size, size), bf16),
            jax.ShapeDtypeStruct((8, 128), f32),
        ],
        in_specs=[VMEM] * 2,
        out_specs=[VMEM] * 4,
        scratch_shapes=[pltpu.SemaphoreType.DMA((4,)), pltpu.SemaphoreType.DMA((4,))],
        compiler_params=pltpu.CompilerParams(collective_id=0, has_side_effects=True),
        name="entry",
    )(own, right_row)
    even_row = jnp.where(is_left, right_row, left_row)
    odd_row = jnp.where(is_left, sib_row, right_row)
    target = float(sector_count * blocks * size * size)
    group = 2 * blocks
    return pl.pallas_call(
        functools.partial(step_kernel, sites // 2, blocks, target),
        out_shape=jax.ShapeDtypeStruct(site_tensors.shape, bf16),
        in_specs=[VMEM] * 7,
        out_specs=VMEM,
        scratch_shapes=[
            pltpu.VMEM((3, 2, size, size), bf16),
            pltpu.VMEM((3, size, size), bf16),
            pltpu.VMEM((3, size, size), bf16),
            pltpu.VMEM((2, 2 * size, 2 * size), bf16),
            pltpu.VMEM((2, size, 2 * size), f32),
            pltpu.VMEM((size, size), f32),
            pltpu.VMEM((size, size), f32),
            pltpu.VMEM((2, 2, size, 2 * size), bf16),
            pltpu.VMEM((2, 2, size, 2 * size), bf16),
            pltpu.VMEM((3, size, 2 * size), bf16),
            pltpu.VMEM((size, 2 * size), bf16),
            pltpu.VMEM((4, size, 2 * size), bf16),
            pltpu.VMEM((2, size, 2 * size), bf16),
            pltpu.VMEM((size, size), bf16),
            pltpu.VMEM((8, 128), f32),
            pltpu.VMEM((2, group, 8, 128), f32),
            pltpu.VMEM((8, 128), f32),
            pltpu.VMEM((8, 128), f32),
            pltpu.SemaphoreType.DMA((12,)),
            pltpu.SemaphoreType.DMA((12,)),
            pltpu.SemaphoreType.DMA((2, group)),
            pltpu.SemaphoreType.DMA((2, group)),
        ],
        compiler_params=pltpu.CompilerParams(collective_id=1, has_side_effects=True),
        name="step",
    )(even_row, odd_row, own, other, outer, lower, sketch.T)


def solution(mesh):
    placed = (
        P("chain", "block", None, None, None),
        P(),
        P("chain", None, None),
        P("chain", None, None),
        P("chain", None, None),
    )
    return jax.shard_map(
        functools.partial(body, mesh.shape["chain"], mesh.shape["block"]),
        mesh=mesh,
        in_specs=placed,
        out_specs=P("chain", "block", None, None, None),
        check_vma=False,
    )
```

profile of v0, /device:TPU:32, one launch (start us, length us, event | category | flops | bytes accessed | tf_op | source)
XLA Modules:
  0.0 200.3 jit_solution(14308667886262893192)
XLA Ops:
  0.0 0.0 copy-start
  0.0 0.8 convert_bitcast_fusion
  0.8 0.8 fusion.1
  1.6 0.1 dynamic-slice_bitcast_fusion
  1.7 0.1 iota_compare_fusion.2
  1.7 0.1 pad_add_fusion
  1.8 0.1 fusion.3
  1.9 0.1 iota_compare_fusion
  2.0 0.9 multiply_exponential_fusion.2
  2.9 0.1 maximum_bitcast_fusion
  2.9 0.1 pad_maximum_fusion
  3.0 0.6 broadcast_in_dim.6.even_row
  3.6 0.6 broadcast_in_dim.8.row
  4.2 1.8 copy.6
  6.0 0.3 broadcast_and_fusion.1
  6.3 0.0 copy-done
  6.3 1.1 add_select_fusion.own
  7.4 14.1 %entry.1 = (bf16[3,2,256,256]{3,2,1,0:T(8,128)(2,1)}, bf16[2,256,256]{2,1,0:T(8,128)(2,1)}, bf16[256,256]{1,0:T(8,128)(2,1)}, f32[8,128]{1,0:T(8,128)}) custom-call(bf16[4,2,256,256]{3,2,1,0:T(8,128)(2,1)} %add_select_fusion.own, f32[8,128]{1,0:T(8,128)} %broadcast_in_dim.8.row), custom_call_target="tpu_custom_call" | custom-call | tf_op jit(solution)/shard_map/entry/pallas_call | solution.py:480
  21.5 0.0 copy-start.1
  21.5 0.7 copy-done.1
  22.2 0.6 broadcast_select_fusion.odd_row
  22.8 175.2 %step.1 = bf16[1,4,2,256,256]{4,3,2,1,0:T(8,128)(2,1)} custom-call(f32[8,128]{1,0:T(8,128)} %broadcast_in_dim.6.even_row, f32[8,128]{1,0:T(8,128)} %broadcast_select_fusion.odd_row, bf16[4,2,256,256]{3,2,1,0:T(8,128)(2,1)} %add_select_fusion.own, bf16[3,2,256,256]{3,2,1,0:T(8,128)(2,1)} %get-tuple-element.10.other, ...), custom_call_target="tpu_custom_call" | custom-call | tf_op jit(solution)/shard_map/step/pallas_call | solution.py:498
  198.0 2.3 %copy.8 = bf16[1,4,2,256,256]{4,3,2,1,0:T(8,128)(2,1)} copy(bf16[1,4,2,256,256]{4,3,2,1,0:T(8,128)(2,1)} %step.1) | data formatting | bytes 2097152
  (2 shorter events, 0.0 us)
Async XLA Ops:
  0.0 6.3 %copy-start = (bf16[1,4,2,256,256]{4,3,2,1,0:T(8,128)(2,1)S(1)}, bf16[1,4,2,256,256]{4,3,2,1,0:T(8,128)(2,1)}, u32[]{:S(2)}) copy-start(bf16[1,4,2,256,256]{4,3,2,1,0:T(8,128)(2,1)} %param.5) | copy-start | bytes 3145732
  21.5 0.7 copy-start.1
where the time goes:
time: 201 us; the launch traced here: 200 us
  Pallas kernels  189 us (94%)
  local copies, waits for them, and re-layouts  6.84 us (3%)
  other arithmetic  4.09 us (2%)
    pallas_call x1, Pallas kernels, body(): pl.pallas_call(functools.partial(step_kernel, sites // 2, blocks, target)...  175 us
    pallas_call x1, Pallas kernels, body(): pl.pallas_call(functools.partial(entry_kernel, blocks), out_shape=[jax.Sh...  14.1 us
    unnamed x6, local copies, waits for them, and re-layouts  4.74 us

commit v1 on v0

--- a/solution.py
+++ b/solution.py
@@ -29,39 +29,49 @@
     return mm(x_high, y_high, dims) + (mm(x_high, y_low, dims) + mm(x_low, y_high, dims))
 
 
+def across(x):
+    return jnp.broadcast_to(x, (8, 128))
+
+
 def inv_factors(blocks):
     nb = blocks[0].shape[0]
-    ngr = nb // 8
-    eye = (lax.broadcasted_iota(jnp.int32, (nb, nb), 0) == lax.broadcasted_iota(jnp.int32, (nb, nb), 1)).astype(jnp.float32)
+    groups = nb // 8
+    eye = lax.broadcasted_iota(jnp.int32, (nb, nb), 0) == lax.broadcasted_iota(jnp.int32, (nb, nb), 1)
+    eye = eye.astype(jnp.float32)
+    sub = lax.broadcasted_iota(jnp.int32, (8, 128), 0)
+    one = jnp.ones((8, 128), jnp.float32)
     work = []
-    for g in blocks:
-        full = jnp.concatenate([g, eye], axis=1)
-        work.append([full[8 * i: 8 * i + 8, :] for i in range(ngr)])
-    lane = lax.broadcasted_iota(jnp.int32, (8, 2 * nb), 1)
-    sub = lax.broadcasted_iota(jnp.int32, (8, 2 * nb), 0)
-    for j in range(nb):
-        gj, sj = j // 8, j % 8
+    for block in blocks:
+        full = jnp.concatenate([block, eye], axis=1)
+        work.append([full[8 * i : 8 * i + 8, :] for i in range(groups)])
+    for g in range(groups):
+        first = 8 * g
+        states = []
         for w in work:
-            row = w[gj][sj: sj + 1, :]
-            piv = row[:, j: j + 1]
-            t = row * (1.0 / piv)
-            tb = jnp.broadcast_to(t, (8, 2 * nb))
-            for i in range(gj, ngr):
-                if i == gj and sj == 7:
-                    continue
-                c = jnp.broadcast_to(w[i][:, j: j + 1], (8, 2 * nb))
-                if i == gj:
-                    c = jnp.where(sub > sj, c, 0.0)
-                w[i] = w[i] - c * tb
-    out = []
-    for w in work:
-        rows = []
-        for i in range(ngr):
-            d = jnp.sum(jnp.where(lane == sub + 8 * i, w[i], 0.0), axis=1, keepdims=True)
-            rows.append(w[i] * lax.rsqrt(d))
-        full = jnp.concatenate(rows, axis=0)
-        out.append(full[:, nb:])
-    return out
+            cols = [across(w[g][:, first + p : first + p + 1]) for p in range(8)]
+            states.append([w[g], w[g], cols, one, one])
+        for p in range(8):
+            for state in states:
+                rows, solved, cols, pivots, inverses = state
+                pivot = across(cols[p][p : p + 1, :])
+                inverse = 1.0 / pivot
+                factor = jnp.where(sub == p, 0.0, cols[p]) * inverse
+                for q in range(p + 1, 8):
+                    cols[q] = cols[q] - factor * across(cols[q][p : p + 1, :])
+                state[0] = rows - jnp.where(sub > p, factor, 0.0) * across(rows[p : p + 1, :])
+                state[1] = solved - factor * across(solved[p : p + 1, :])
+                state[3] = jnp.where(sub == p, pivot, pivots)
+                state[4] = jnp.where(sub == p, inverse, inverses)
+        for w, (rows, solved, cols, pivots, inverses) in zip(work, states):
+            w[g] = rows * lax.rsqrt(pivots)
+            solved = solved * inverses
+            spread = [across(solved[p : p + 1, :]) for p in range(8)]
+            for i in range(g + 1, groups):
+                terms = [across(w[i][:, first + p : first + p + 1]) * spread[p] for p in range(8)]
+                terms = [terms[k] + terms[k + 1] for k in range(0, 8, 2)]
+                w[i] = w[i] - ((terms[0] + terms[1]) + (terms[2] + terms[3]))
+    return [jnp.concatenate(w, axis=0)[:, nb:] for w in work]
+
 
 def inv_cholesky(w_refs, nb=64, mmf=mm3):
     n = w_refs[0].shape[-1]
@@ -88,19 +98,6 @@
 
 MESH = pl.DeviceIdType.MESH
 VMEM = pl.BlockSpec(memory_space=pltpu.VMEM)
-
-
-def gate_terms(coupling):
-    hopping = coupling[0]
-    ising_term = coupling[1]
-    field_term = coupling[2]
-    rotation = 0.5 * tau_step * hopping
-    middle_scale = jnp.exp(0.25 * tau_step * ising_term)
-    weight_empty = jnp.exp(-tau_step * (0.25 * ising_term - 0.5 * field_term))
-    weight_full = jnp.exp(-tau_step * (0.25 * ising_term + 0.5 * field_term))
-    weight_stay = middle_scale * jnp.cosh(rotation)
-    weight_swap = -middle_scale * jnp.sinh(rotation)
-    return jnp.stack([weight_empty, weight_stay, weight_swap, weight_full])
 
 
 def update_sectors(left, top, low, bdims, sketch_t, ranks, weights, basis_ref, coef_ref, part_ref, scratch, sent):
@@ -151,11 +148,14 @@
     pl.semaphore_signal(semaphore, inc=1, device_id={"chain": chain, "block": block}, device_id_type=MESH)
 
 
-def entry_kernel(blocks, own, row, other, outer, lower, sib_row, send_sems, recv_sems):
+def entry_kernel(blocks, own, sketch, sizes, counts, terms, left, top, low, sketch_t, even_row, odd_row, *refs):
+    (other, outer, lower, sib_sizes, sib_counts, sib_terms, send_sems, recv_sems) = refs
+    size = outer.shape[-1]
     chain = lax.axis_index("chain")
     block = lax.axis_index("block")
     side = lax.rem(chain, 2)
     sib = chain + 1 - 2 * side
+    first = block * own.shape[1] + side * 2
     has_prev = block > 0
     has_next = block < blocks - 1
     even = side == 0
@@ -180,16 +180,21 @@
             device_id_type=MESH,
         )
 
-    edge_next = remote(own.at[3], outer, 0, chain, block + 1)
-    edge_prev = remote(own.at[0], outer, 0, chain, block - 1)
-    edge_low = remote(own.at[3, 1], lower, 1, sib, block + 1)
-    to_odd = remote(own.at[pl.ds(1, 3)], other, 2, sib, block)
-    to_even = remote(own.at[pl.ds(0, 3)], other, 2, sib, block)
-    rows = remote(row, sib_row, 3, sib, block)
+    edge_next = remote(own.at[0, 3], outer, 0, chain, block + 1)
+    edge_prev = remote(own.at[0, 0, 0], outer.at[0], 1, chain, block - 1)
+    edge_low = remote(own.at[0, 3, 1], lower, 2, sib, block + 1)
+    to_odd = remote(own.at[0, pl.ds(1, 3)], other, 3, sib, block)
+    to_even = remote(own.at[0, pl.ds(0, 3)], other, 3, sib, block)
+    rows = [
+        remote(sizes, sib_sizes, 4, sib, block),
+        remote(counts, sib_counts, 5, sib, block),
+        remote(terms, sib_terms, 6, sib, block),
+    ]
     pl.when(even & has_next)(edge_next.start)
+    pl.when(odd & has_next)(edge_low.start)
     pl.when(odd & has_prev)(edge_prev.start)
-    pl.when(odd & has_next)(edge_low.start)
-    rows.start()
+    for copy in rows:
+        copy.start()
     pl.when(even)(to_odd.start)
     pl.when(odd)(to_even.start)
 
@@ -197,21 +202,102 @@
     def _():
         outer[...] = jnp.zeros_like(outer)
 
-    @pl.when(odd | (block == 0))
+    @pl.when(even & (block == 0))
     def _():
         lower[...] = jnp.zeros_like(lower)
 
-    rows.wait()
-    to_odd.wait()
-    pl.when((even & has_prev) | (odd & has_next))(edge_next.wait_recv)
-    pl.when((even & has_next) | (odd & has_prev))(edge_next.wait_send)
-    pl.when(even & has_prev)(edge_low.wait_recv)
-    pl.when(odd & has_next)(edge_low.wait_send)
-
-
-def step_kernel(chips, blocks, target, even_row, odd_row, own, other, outer, lower, sketch_t, out, *refs):
-    (left_ref, top_ref, low_ref, two_ref, sample_ref, tri_a, tri_b, basis_ref, coef_ref, far_ref, edge_ref) = refs[:11]
-    (new_ref, sib_ref, bot_ref, part_ref, norm_ref, sum_ref, scale_ref, send_sems, recv_sems, nsend, nrecv) = refs[11:]
+    sketch_t[...] = sketch[...].astype(jnp.float32).T.astype(jnp.bfloat16)
+    for copy in rows:
+        copy.wait()
+
+    def entry(row, index):
+        lane = lax.broadcasted_iota(jnp.int32, row.shape, 1)
+        return jnp.sum(jnp.where(lane == index, row.astype(jnp.float32), 0.0), axis=1, keepdims=True)
+
+    def write_row(ref, count_row, term_row):
+        hopping, ising, field = (term_row[:, i : i + 1] for i in range(3))
+        rotation = 0.5 * tau_step * hopping
+        middle = jnp.exp(0.25 * tau_step * ising)
+        grow, shrink = jnp.exp(rotation), jnp.exp(-rotation)
+        values = [
+            entry(count_row, first),
+            entry(count_row, first + 1),
+            jnp.exp(-tau_step * (0.25 * ising - 0.5 * field)),
+            middle * (0.5 * (grow + shrink)),
+            -middle * (0.5 * (grow - shrink)),
+            jnp.exp(-tau_step * (0.25 * ising + 0.5 * field)),
+        ]
+        lane = lax.broadcasted_iota(jnp.int32, ref.shape, 1)
+        result = jnp.zeros(ref.shape, jnp.float32)
+        for i, value in enumerate(values):
+            result = jnp.where(lane == i, jnp.broadcast_to(value, ref.shape), result)
+        ref[...] = result
+
+    def pick(take, first_row, second_row):
+        return jnp.where(take, first_row.astype(jnp.float32), second_row.astype(jnp.float32))
+
+    write_row(
+        even_row,
+        pick(even, counts[0, 1:2, :], counts[0, 0:1, :]),
+        pick(even, terms[0, 1:2, :], terms[0, 0:1, :]),
+    )
+    write_row(
+        odd_row,
+        pick(odd, counts[0, 1:2, :], sib_counts[0, 1:2, :]),
+        pick(odd, terms[0, 1:2, :], sib_terms[0, 1:2, :]),
+    )
+    lefts = [pick(even, sizes[0, i : i + 1, :], sib_sizes[0, i : i + 1, :]) for i in range(2)]
+    rights = [pick(odd, sizes[0, i : i + 1, :], sib_sizes[0, i : i + 1, :]) for i in range(2)]
+    row = lax.broadcasted_iota(jnp.int32, (size, size), 0).astype(jnp.float32)
+    column = lax.broadcasted_iota(jnp.int32, (size, size), 1).astype(jnp.float32)
+
+    def cut(value, bond, sector, shift):
+        keep = (row < entry(bond[0], sector)) & (column < entry(bond[1], sector + shift))
+        return jnp.where(keep, value.astype(jnp.float32), 0.0).astype(jnp.bfloat16)
+
+    def put_left(k, value):
+        for s in range(2):
+            left[k, s] = cut(value(s), lefts, first - 1 + k, s)
+
+    def put_top(k, value):
+        top[k] = cut(value, rights, first + k, 0)
+
+    def put_low(k, value):
+        low[k] = cut(value, rights, first - 1 + k, 1)
+
+    @pl.when(even)
+    def _():
+        put_left(1, lambda s: own[0, 0, s])
+        put_left(2, lambda s: own[0, 1, s])
+        to_odd.wait()
+        for i in range(3):
+            put_top(i, other[i, 0])
+        for i in range(2):
+            put_low(i + 1, other[i, 1])
+        pl.when(has_prev)(edge_next.wait_recv)
+        pl.when(has_prev)(edge_low.wait_recv)
+        put_left(0, lambda s: outer[s])
+        put_low(0, lower[...])
+        pl.when(has_next)(edge_next.wait_send)
+
+    @pl.when(odd)
+    def _():
+        for i in range(3):
+            put_low(i, own[0, i + 1, 1])
+        for i in range(2):
+            put_top(i, own[0, i + 2, 0])
+        to_even.wait()
+        for i in range(3):
+            put_left(i, lambda s: other[i, s])
+        pl.when(has_next)(edge_prev.wait_recv)
+        put_top(2, outer[0])
+        pl.when(has_prev)(edge_prev.wait_send)
+        pl.when(has_next)(edge_low.wait_send)
+
+
+def step_kernel(chips, blocks, target, left_ref, top_ref, low_ref, sketch_t, even_row, odd_row, out, *refs):
+    (two_ref, sample_ref, tri_a, tri_b, basis_ref, coef_ref, far_ref, edge_ref) = refs[:8]
+    (sib_ref, bot_ref, part_ref, norm_ref, sum_ref, scale_ref, send_sems, recv_sems, nsend, nrecv, turn) = refs[8:]
     size = bot_ref.shape[0]
     chain = lax.axis_index("chain")
     block = lax.axis_index("block")
@@ -294,26 +380,6 @@
             total = total + norm_ref[layer, i]
         return jnp.sqrt(target / total)
 
-    @pl.when(even)
-    def _():
-        left_ref[0] = outer[...]
-        left_ref[1] = own[0]
-        left_ref[2] = own[1]
-        low_ref[0] = lower[...]
-        for i in range(3):
-            top_ref[i] = other[i, 0]
-        for i in range(2):
-            low_ref[i + 1] = other[i, 1]
-
-    @pl.when(odd)
-    def _():
-        for i in range(3):
-            left_ref[i] = other[i]
-            low_ref[i] = own[i + 1, 1]
-        for i in range(2):
-            top_ref[i] = own[i + 2, 0]
-        top_ref[2] = outer[0]
-
     @pl.when(even & (block == 0))
     def _():
         edge_ref[...] = jnp.zeros_like(edge_ref)
@@ -327,9 +393,8 @@
         bot_ref[...] = jnp.zeros_like(bot_ref)
 
     def row_terms(ref):
-        terms = [ref[0:1, i : i + 1] for i in range(8)]
-        ranks = [jnp.where(even, terms[i], terms[i + 2]) for i in range(2)]
-        return ranks, terms[4:]
+        terms = [ref[0:1, i : i + 1] for i in range(6)]
+        return terms[:2], terms[2:]
 
     far = [remote(basis_ref.at[0, i], far_ref.at[i], i, back, block) for i in range(2)]
     edge_even = remote(coef_ref.at[0, 1], edge_ref, 2, sib, block)
@@ -341,7 +406,7 @@
         if i == 0:
             pl.semaphore_wait(barrier, group + 2)
             far[0].start()
-            far[1].start()
+            pl.when(even)(far[1].start)
         else:
             pl.when(even)(edge_even.start)
             pl.when(odd & has_next)(edge_odd.start)
@@ -366,6 +431,18 @@
     far[0].wait_recv()
     pl.when(even & has_prev)(pass_even.start)
     pl.when(odd)(pass_odd.start)
+    far[0].wait_send()
+
+    @pl.when(even)
+    def _():
+        far[1].wait_send()
+        signal_to(turn, sib, block)
+
+    @pl.when(odd)
+    def _():
+        pl.semaphore_wait(turn, 1)
+        far[1].start()
+
     scale = norm_scale(0)[0:1, 0:1]
     pl.when(odd | has_prev)(edge_even.wait_recv)
     far[1].wait_recv()
@@ -373,14 +450,20 @@
 
     lefts = (edge_ref, coef_ref.at[0, 0], coef_ref.at[0, 1])
     ranks, weights = row_terms(odd_row)
-    new_even = [remote(coef_ref.at[1, i], new_ref.at[i], 4 + i, ahead, block) for i in range(2)]
-    new_odd = [remote(coef_ref.at[1, i], new_ref.at[2 + i], 6 + i, ahead_even, block) for i in range(2)]
-    sibs = [remote(basis_ref.at[1, i], sib_ref.at[i], 8 + i, sib, block) for i in range(2)]
-    bot = remote(basis_ref.at[1, 0, :, pl.ds(size, size)], bot_ref, 10, sib, block - 1)
+    new_even, new_odd = [], []
+    for i in range(2):
+        for half in range(2):
+            piece = coef_ref.at[1, i, :, pl.ds(half * size, size)]
+            k = 2 * i + half
+            new_even.append(remote(piece, out.at[0, i, half], 4 + k, ahead, block))
+            new_odd.append(remote(piece, out.at[0, 2 + i, half], 8 + k, ahead_even, block))
+    sibs = [remote(basis_ref.at[1, i], sib_ref.at[i], 12 + i, sib, block) for i in range(2)]
+    bot = remote(basis_ref.at[1, 0, :, pl.ds(size, size)], bot_ref, 14, sib, block - 1)
 
     def sent_odd(i):
-        pl.when(even)(new_even[i].start)
-        pl.when(odd)(new_odd[i].start)
+        for k in (2 * i, 2 * i + 1):
+            pl.when(even)(new_even[k].start)
+            pl.when(odd)(new_odd[k].start)
         pl.when(even)(sibs[i].start)
         if i == 1:
             pl.when(even & has_prev)(bot.start)
@@ -401,20 +484,19 @@
     )
     share_norm(1)
     sum_ref[...] = norm_scale(1)
-    scale_copy = remote(sum_ref, scale_ref, 11, ahead, block)
+    scale_copy = remote(sum_ref, scale_ref, 15, ahead, block)
     pl.when(even)(scale_copy.start)
 
     @pl.when(even)
     def _():
-        for i in range(2):
-            new_even[i].wait_recv()
-            new_odd[i].wait_recv()
+        for k in range(4):
+            new_even[k].wait_recv()
+            new_odd[k].wait_recv()
         scale_copy.wait_recv()
         scale = scale_ref[0:1, 0:1]
         for i in range(4):
-            scaled = (new_ref[i].astype(jnp.float32) * scale).astype(jnp.bfloat16)
-            out[0, i, 0] = scaled[:, :size]
-            out[0, i, 1] = scaled[:, size:]
+            for half in range(2):
+                out[0, i, half] = (out[0, i, half].astype(jnp.float32) * scale).astype(jnp.bfloat16)
 
     @pl.when(odd)
     def _():
@@ -431,10 +513,11 @@
                 out[0, i - 1, 1] = flip(basis[:, size:])
         out[0, 3, 1] = flip(bot_ref[...])
 
+    pl.when(odd)(far[1].wait_send)
+    for k in range(4):
+        pl.when(even)(new_even[k].wait_send)
+        pl.when(odd)(new_odd[k].wait_send)
     for i in range(2):
-        far[i].wait_send()
-        pl.when(even)(new_even[i].wait_send)
-        pl.when(odd)(new_odd[i].wait_send)
         pl.when(even)(sibs[i].wait_send)
     pl.when(even | has_next)(edge_even.wait_send)
     pl.when(odd | has_prev)(pass_even.wait_send)
@@ -445,65 +528,45 @@
             norm_copy(layer, step).wait_send()
 
 
-def local_mask(site_block, sizes_row, first_sector):
-    sector_count = site_block.shape[0]
-    block_width = site_block.shape[-1]
-    right_ext = jnp.concatenate([sizes_row[1], jnp.zeros((1,), jnp.int32)])
-    left_here = lax.dynamic_slice_in_dim(sizes_row[0], first_sector, sector_count)
-    right_here = lax.dynamic_slice_in_dim(right_ext, first_sector, sector_count)
-    right_next = lax.dynamic_slice_in_dim(right_ext, first_sector + 1, sector_count)
-    row_index = jnp.arange(block_width, dtype=jnp.int32)
-    row_keep = row_index[None, :] < left_here[:, None]
-    col_stay = row_index[None, :] < right_here[:, None]
-    col_next = row_index[None, :] < right_next[:, None]
-    keep_zero = row_keep[:, :, None] & col_stay[:, None, :]
-    keep_one = row_keep[:, :, None] & col_next[:, None, :]
-    keep_both = jnp.stack([keep_zero, keep_one], axis=1)
-    return jnp.where(keep_both, site_block, jnp.zeros_like(site_block))
-
-
 def body(sites, blocks, site_tensors, sketch, bond_sizes, kept_ranks, couplings):
     sector_count = site_tensors.shape[1]
     size = site_tensors.shape[-1]
     bf16 = jnp.bfloat16
     f32 = jnp.float32
-    chain = lax.axis_index("chain")
-    block = lax.axis_index("block")
-    is_left = lax.rem(chain, 2) == 0
-    first_sector = block * sector_count
-
-    counts = lax.dynamic_slice_in_dim(kept_ranks[0], first_sector, sector_count, axis=1).astype(f32)
-    rows = jnp.concatenate([counts, gate_terms(couplings[0].T).T], axis=1)
-    left_row, right_row = (jnp.broadcast_to(jnp.pad(rows[i], (0, 120))[None], (8, 128)) for i in range(2))
-    own = local_mask(site_tensors[0], bond_sizes[0], first_sector)
-
-    other, outer, lower, sib_row = pl.pallas_call(
+    row = jax.ShapeDtypeStruct((8, 128), f32)
+    terms = pl.pallas_call(
         functools.partial(entry_kernel, blocks),
         out_shape=[
             jax.ShapeDtypeStruct((3, 2, size, size), bf16),
-            jax.ShapeDtypeStruct((2, size, size), bf16),
-            jax.ShapeDtypeStruct((size, size), bf16),
-            jax.ShapeDtypeStruct((8, 128), f32),
+            jax.ShapeDtypeStruct((3, size, size), bf16),
+            jax.ShapeDtypeStruct((3, size, size), bf16),
+            jax.ShapeDtypeStruct((size, 2 * size), bf16),
+            row,
+            row,
         ],
-        in_specs=[VMEM] * 2,
-        out_specs=[VMEM] * 4,
-        scratch_shapes=[pltpu.SemaphoreType.DMA((4,)), pltpu.SemaphoreType.DMA((4,))],
+        in_specs=[VMEM] * 5,
+        out_specs=[VMEM] * 6,
+        scratch_shapes=[
+            pltpu.VMEM((3, 2, size, size), bf16),
+            pltpu.VMEM((2, size, size), bf16),
+            pltpu.VMEM((size, size), bf16),
+            pltpu.VMEM(bond_sizes.shape, jnp.int32),
+            pltpu.VMEM(kept_ranks.shape, jnp.int32),
+            pltpu.VMEM(couplings.shape, f32),
+            pltpu.SemaphoreType.DMA((7,)),
+            pltpu.SemaphoreType.DMA((7,)),
+        ],
         compiler_params=pltpu.CompilerParams(collective_id=0, has_side_effects=True),
         name="entry",
-    )(own, right_row)
-    even_row = jnp.where(is_left, right_row, left_row)
-    odd_row = jnp.where(is_left, sib_row, right_row)
+    )(site_tensors, sketch, bond_sizes, kept_ranks, couplings)
     target = float(sector_count * blocks * size * size)
     group = 2 * blocks
     return pl.pallas_call(
         functools.partial(step_kernel, sites // 2, blocks, target),
         out_shape=jax.ShapeDtypeStruct(site_tensors.shape, bf16),
-        in_specs=[VMEM] * 7,
+        in_specs=[VMEM] * 6,
         out_specs=VMEM,
         scratch_shapes=[
-            pltpu.VMEM((3, 2, size, size), bf16),
-            pltpu.VMEM((3, size, size), bf16),
-            pltpu.VMEM((3, size, size), bf16),
             pltpu.VMEM((2, 2 * size, 2 * size), bf16),
             pltpu.VMEM((2, size, 2 * size), f32),
             pltpu.VMEM((size, size), f32),
@@ -512,21 +575,21 @@
             pltpu.VMEM((2, 2, size, 2 * size), bf16),
             pltpu.VMEM((3, size, 2 * size), bf16),
             pltpu.VMEM((size, 2 * size), bf16),
-            pltpu.VMEM((4, size, 2 * size), bf16),
             pltpu.VMEM((2, size, 2 * size), bf16),
             pltpu.VMEM((size, size), bf16),
             pltpu.VMEM((8, 128), f32),
             pltpu.VMEM((2, group, 8, 128), f32),
             pltpu.VMEM((8, 128), f32),
             pltpu.VMEM((8, 128), f32),
-            pltpu.SemaphoreType.DMA((12,)),
-            pltpu.SemaphoreType.DMA((12,)),
+            pltpu.SemaphoreType.DMA((16,)),
+            pltpu.SemaphoreType.DMA((16,)),
             pltpu.SemaphoreType.DMA((2, group)),
             pltpu.SemaphoreType.DMA((2, group)),
+            pltpu.SemaphoreType.REGULAR,
         ],
         compiler_params=pltpu.CompilerParams(collective_id=1, has_side_effects=True),
         name="step",
-    )(even_row, odd_row, own, other, outer, lower, sketch.T)
+    )(*terms)
 
 
 def solution(mesh):

time: 201 us -> 166 us (0.83)
  Pallas kernels: 189 us -> 164 us
  local copies, waits for them, and re-layouts: 6.84 us -> 2.26 us
  other arithmetic: 4.09 us -> 0 us
    pallas_call x1, Pallas kernels: 175 us -> 149 us  [body(): pl.pallas_call(functools.partial(step_kernel, sites // 2, blocks, target)...]
    unnamed x6 -> x1, local copies, waits for them, and re-layouts: 4.74 us -> 2.26 us
where the time goes in v1:
time: 166 us
  Pallas kernels  164 us (99%)
  local copies, waits for them, and re-layouts  2.26 us (1%)
    pallas_call x1, Pallas kernels, body(): pl.pallas_call(functools.partial(step_kernel, sites // 2, blocks, target)...  149 us
    pallas_call x1, Pallas kernels, body(): pl.pallas_call(functools.partial(entry_kernel, blocks), out_shape=[jax.Sh...  14.6 us

profile of v1, /device:TPU:32, one launch (start us, length us, event | category | flops | bytes accessed | tf_op | source)
XLA Modules:
  0.0 166.1 jit_solution(6604885643169881148)
XLA Ops:
  0.0 14.6 %entry.1 = (bf16[3,2,256,256]{3,2,1,0:T(8,128)(2,1)}, bf16[3,256,256]{2,1,0:T(8,128)(2,1)}, bf16[3,256,256]{2,1,0:T(8,128)(2,1)}, bf16[256,512]{1,0:T(8,128)(2,1)}, f32[8,128]{1,0:T(8,128)}, /*index=5*/f32[8,128]{1,0:T(8,128)}) custom-call(bf16[1,4,2,256,256]{4,3,2,1,0:T(8,128)(2,1)} %own.1, bf16[512,256]{1,0:T(8,128)(2,1)} %sketch.1, s32[1,2,32]{2,1,0:T(2,128)} %sizes.1, ...), custom_call_target="tpu_custom_call" | custom-call | tf_op jit(solution)/shard_map/entry/pallas_call | solution.py:537
  14.7 149.2 %step.1 = bf16[1,4,2,256,256]{4,3,2,1,0:T(8,128)(2,1)} custom-call(bf16[3,2,256,256]{3,2,1,0:T(8,128)(2,1)} %get-tuple-element.11.left_ref, bf16[3,256,256]{2,1,0:T(8,128)(2,1)} %get-tuple-element.12.top_ref, bf16[3,256,256]{2,1,0:T(8,128)(2,1)} %get-tuple-element.13.low_ref, bf16[256,512]{1,0:T(8,128)(2,1)} %get-tuple-element.14.sketch_t, ...), custom_call_target="tpu_custom_call" | custom-call | tf_op jit(solution)/shard_map/step/pallas_call | solution.py:564
  163.9 2.3 %copy.7 = bf16[1,4,2,256,256]{4,3,2,1,0:T(8,128)(2,1)} copy(bf16[1,4,2,256,256]{4,3,2,1,0:T(8,128)(2,1)} %step.1) | data formatting | bytes 2097152

commit v2 on v1

--- a/solution.py
+++ b/solution.py
@@ -100,7 +100,7 @@
 VMEM = pl.BlockSpec(memory_space=pltpu.VMEM)
 
 
-def update_sectors(left, top, low, bdims, sketch_t, ranks, weights, basis_ref, coef_ref, part_ref, scratch, sent):
+def update_sectors(left, top, low, bdims, sketch_t, ranks, weights, basis_ref, coef_ref, part_ref, scratch, before, sent):
     two_ref, sample_ref, tri_refs = scratch
     w_empty, w_stay, w_swap, w_full = weights
     size = sample_ref.shape[1]
@@ -108,9 +108,15 @@
     def product(x, y):
         return mm(x, y, bdims).astype(jnp.bfloat16).astype(jnp.float32)
 
-    up_stay = product(left(0, 1), top(0))
-    stay_up = product(left(0, 0), low(0))
+    row = lax.broadcasted_iota(jnp.int32, (size, size), 0)
+    column = lax.broadcasted_iota(jnp.int32, (size, size), 1)
+    row_wide = lax.broadcasted_iota(jnp.int32, (size, 2 * size), 0)
+    total = jnp.zeros((1, 1), jnp.float32)
     for i in range(2):
+        before(i)
+        if i == 0:
+            up_stay = product(left(0, 1), top(0))
+            stay_up = product(left(0, 0), low(0))
         up_up = product(left(i, 1), low(i + 1))
         two_ref[i, size:, :size] = (w_swap * stay_up + w_stay * up_stay).astype(jnp.bfloat16)
         two_ref[i, size:, size:] = (w_full * up_up).astype(jnp.bfloat16)
@@ -119,10 +125,6 @@
         up_stay = product(left(i + 1, 1), top(i + 1))
         two_ref[i, :size, :size] = (w_empty * stay_stay).astype(jnp.bfloat16)
         two_ref[i, :size, size:] = (w_stay * stay_up + w_swap * up_stay).astype(jnp.bfloat16)
-    row = lax.broadcasted_iota(jnp.int32, (size, size), 0)
-    column = lax.broadcasted_iota(jnp.int32, (size, size), 1)
-    row_wide = lax.broadcasted_iota(jnp.int32, (size, 2 * size), 0)
-    for i in range(2):
         sample = mm(sketch_t[...], two_ref[i], NT)
         sample = jnp.where(row_wide.astype(jnp.float32) < ranks[i], sample, 0.0)
         sample_ref[i] = sample
@@ -131,12 +133,9 @@
         gram = mm(high, high, NT) + (cross + cross.T)
         free = (row == column) & (row.astype(jnp.float32) >= ranks[i])
         tri_refs[i][...] = gram + jnp.where(free, 1.0, 0.0)
-    inv_cholesky(tri_refs)
-    total = jnp.zeros((1, 1), jnp.float32)
-    for i in range(2):
+        inv_cholesky(tri_refs[i : i + 1])
         basis = mm3(tri_refs[i][...], sample_ref[i]) * math.sqrt(size)
         basis_ref[i] = basis.astype(jnp.bfloat16)
-    for i in range(2):
         coef = mm(basis_ref[i], two_ref[i])
         total = total + jnp.sum(jnp.sum(coef * coef, axis=1, keepdims=True), axis=0, keepdims=True)
         coef_ref[i] = coef.astype(jnp.bfloat16)
@@ -402,12 +401,19 @@
     pass_even = remote(far_ref.at[0], far_ref.at[2], 3, sib, block - 1)
     pass_odd = remote(far_ref.at[0], far_ref.at[2], 3, sib, block)
 
+    first_turn = even
+
+    def before_even(i):
+        pass
+
     def sent_even(i):
         if i == 0:
             pl.semaphore_wait(barrier, group + 2)
-            far[0].start()
-            pl.when(even)(far[1].start)
+        if i == 0:
+            far[i].start()
         else:
+            pl.when(first_turn)(far[i].start)
+        if i == 1:
             pl.when(even)(edge_even.start)
             pl.when(odd & has_next)(edge_odd.start)
 
@@ -425,16 +431,17 @@
         coef_ref.at[0],
         part_ref,
         scratch,
+        before_even,
         sent_even,
     )
     share_norm(0)
     far[0].wait_recv()
     pl.when(even & has_prev)(pass_even.start)
     pl.when(odd)(pass_odd.start)
-    far[0].wait_send()
 
     @pl.when(even)
     def _():
+        far[0].wait_send()
         far[1].wait_send()
         signal_to(turn, sib, block)
 
@@ -445,8 +452,12 @@
 
     scale = norm_scale(0)[0:1, 0:1]
     pl.when(odd | has_prev)(edge_even.wait_recv)
-    far[1].wait_recv()
-    pl.when(even | has_next)(pass_even.wait_recv)
+
+    def before_odd(i):
+        if i == 0:
+            far[1].wait_recv()
+        else:
+            pl.when(even | has_next)(pass_even.wait_recv)
 
     lefts = (edge_ref, coef_ref.at[0, 0], coef_ref.at[0, 1])
     ranks, weights = row_terms(odd_row)
@@ -480,6 +491,7 @@
         coef_ref.at[1],
         part_ref,
         scratch,
+        before_odd,
         sent_odd,
     )
     share_norm(1)
@@ -513,6 +525,7 @@
                 out[0, i - 1, 1] = flip(basis[:, size:])
         out[0, 3, 1] = flip(bot_ref[...])
 
+    pl.when(odd)(far[0].wait_send)
     pl.when(odd)(far[1].wait_send)
     for k in range(4):
         pl.when(even)(new_even[k].wait_send)

time: 166 us -> 156 us (0.940)
  Pallas kernels: 164 us -> 153 us
    pallas_call x1, Pallas kernels: 149 us -> 139 us  [body(): pl.pallas_call(functools.partial(step_kernel, sites // 2, blocks, target)...]
where the time goes in v2:
time: 156 us
  Pallas kernels  153 us (98%)
  local copies, waits for them, and re-layouts  2.26 us (1%)
    pallas_call x1, Pallas kernels, body(): pl.pallas_call(functools.partial(step_kernel, sites // 2, blocks, target)...  139 us
    pallas_call x1, Pallas kernels, body(): pl.pallas_call(functools.partial(entry_kernel, blocks), out_shape=[jax.Sh...  14.6 us

profile of v2, /device:TPU:32, one launch (start us, length us, event | category | flops | bytes accessed | tf_op | source)
XLA Modules:
  0.0 155.6 jit_solution(14996385726081709384)
XLA Ops:
  0.0 14.6 %entry.1 = (bf16[3,2,256,256]{3,2,1,0:T(8,128)(2,1)}, bf16[3,256,256]{2,1,0:T(8,128)(2,1)}, bf16[3,256,256]{2,1,0:T(8,128)(2,1)}, bf16[256,512]{1,0:T(8,128)(2,1)}, f32[8,128]{1,0:T(8,128)}, /*index=5*/f32[8,128]{1,0:T(8,128)}) custom-call(bf16[1,4,2,256,256]{4,3,2,1,0:T(8,128)(2,1)} %own.1, bf16[512,256]{1,0:T(8,128)(2,1)} %sketch.1, s32[1,2,32]{2,1,0:T(2,128)} %sizes.1, ...), custom_call_target="tpu_custom_call" | custom-call | tf_op jit(solution)/shard_map/entry/pallas_call | solution.py:550
  14.7 138.7 %step.1 = bf16[1,4,2,256,256]{4,3,2,1,0:T(8,128)(2,1)} custom-call(bf16[3,2,256,256]{3,2,1,0:T(8,128)(2,1)} %get-tuple-element.11.left_ref, bf16[3,256,256]{2,1,0:T(8,128)(2,1)} %get-tuple-element.12.top_ref, bf16[3,256,256]{2,1,0:T(8,128)(2,1)} %get-tuple-element.13.low_ref, bf16[256,512]{1,0:T(8,128)(2,1)} %get-tuple-element.14.sketch_t, ...), custom_call_target="tpu_custom_call" | custom-call | tf_op jit(solution)/shard_map/step/pallas_call | solution.py:577
  153.3 2.3 %copy.7 = bf16[1,4,2,256,256]{4,3,2,1,0:T(8,128)(2,1)} copy(bf16[1,4,2,256,256]{4,3,2,1,0:T(8,128)(2,1)} %step.1) | data formatting | bytes 2097152
